TPU v7x, 32 devices: a whole 2x2x4 slice. The times are simulated.
32 devices in a mesh: sweep: 4 (over x, core), bulk: 8 (over z, y).
Axes of the slice: x: 2, y: 2, z: 4, core: 2. Of those that a mesh axis runs over, the one named last changes fastest.
Arguments:
- source: float32 [128, 5, 128, 128], P('sweep', None, 'bulk'), may hold values from -6 to 6
- psi_old: float32 [128, 5, 128, 128], P('sweep', None, 'bulk'), may hold values from -6 to 6
- lateral: float32 [128, 2, 128, 128], P('sweep', None, 'bulk'), may hold values from 0.1 to 0.6
- lower_jac: float32 [128, 5, 5, 128, 128], P('sweep', None, None, 'bulk')
- upper_jac: float32 [128, 5, 5, 128, 128], P('sweep', None, None, 'bulk')
- diag_inv: float32 [128, 5, 5, 128, 128], P('sweep', None, None, 'bulk')
- face_weight: float32 [5, 65536], P(None, ('sweep', 'bulk')), may hold values from -6 to 6
- face_cell: int32 [65536], P(('sweep', 'bulk')), may hold values from 0 to 65535
- face_owner: int32 [65536, 1], P(('sweep', 'bulk')), may hold values from 0 to 7; in each aligned block of 2048 rows (0 to 2047, 2048 to 4095, ...) at most 512 rows name the same one
- face_node: int32 [65536], P(('sweep', 'bulk')), may hold values from 0 to 16383
- face_count: int32 [32], P(('sweep', 'bulk')), may hold values from 1 to 2048, as said below
Outputs:
- adjoint: float32 [128, 5, 128, 128], P('sweep', None, 'bulk')
- node_sens: float32 [131072], P('bulk')
Inputs may be any that keep to these rules, and one draw needn't show every extreme that they name: `face_owner`: among the 2048 faces of one device no owner appears more than 512 times; some device reaches 512. `face_count`: some device has all 2048 slots live.
All inputs are finite; a program needn't handle non-finite values.
Results may differ from a plain program's by a relative error of at most 0.00011.
Values sent between devices are 32-bit elements; how exact they have to be, the bound alone decides.
No kernel may reach another device: no remote copies, remote signals or barrier semaphores. Data moves between devices by JAX's collectives and lax.ppermute only.
A program may use at most 128 MiB of HBM per device.

v0:
```python
import jax
import jax.numpy as jnp
from jax import lax
from jax.sharding import PartitionSpec as P

NODES_DEV = 16384


def padded_2(value, sides, width):
    for axis, dim in sides:
        size, length = (lax.axis_size(axis), value.shape[dim])
        up = [(i, (i + 1) % size) for i in range(size - 1)]
        down = [(j, i) for i, j in up]
        last = lax.slice_in_dim(value, length - width, length, axis=dim)
        initial = lax.slice_in_dim(value, 0, width, axis=dim)
        before = lax.ppermute(last, axis, up)
        after = lax.ppermute(initial, axis, down)
        value = jnp.concatenate([before, value, after], axis=dim)
    return value


def from_behind(value, axis, by):
    length = lax.axis_size(axis)
    pairs = [(i, i + by) for i in range(length) if 0 <= i + by < length]
    return lax.ppermute(value, axis, pairs)


def matvec(matrix, vector):
    return jnp.sum(matrix * vector[None], axis=1)


def matmat(matrix, other):
    return jnp.sum(matrix[:, :, None] * other[None], axis=1)


def forward_sweep(right_side, lower_jac, diag_inv, start):

    def forward_advance(current, planes):
        rhs_plane, lower_plane, inv_plane = planes
        updated = matvec(inv_plane, rhs_plane - matvec(lower_plane, current))
        return (updated, updated)

    leaving, fields = lax.scan(
        forward_advance, start, (right_side, lower_jac, diag_inv), unroll=True
    )
    return fields


def backward_sweep(forward_field, upper_jac, diag_inv, start):

    def backward_advance(current, planes):
        fwd_plane, upper_plane, inv_plane = planes
        updated = fwd_plane - matvec(inv_plane, matvec(upper_plane, current))
        return (updated, updated)

    leaving, fields = lax.scan(
        backward_advance, start, (forward_field, upper_jac, diag_inv), reverse=True, unroll=True
    )
    return fields


def block_affine(given, coupled, diag_inv, identity, zero_state, backward):

    def block_advance(carry, planes):
        transfer, current = carry
        given_plane, coupled_plane, inv_plane = planes
        transfer = -matmat(inv_plane, matmat(coupled_plane, transfer))
        if backward:
            current = given_plane - matvec(inv_plane, matvec(coupled_plane, current))
        else:
            current = matvec(inv_plane, given_plane - matvec(coupled_plane, current))
        return ((transfer, current), 0)

    result, unused = lax.scan(
        block_advance,
        (identity, zero_state),
        (given, coupled, diag_inv),
        reverse=backward,
        unroll=True,
    )
    return result


def per_device(
    source,
    psi_old,
    lateral,
    lower_jac,
    upper_jac,
    diag_inv,
    face_weight,
    face_cell,
    face_owner,
    face_node,
    face_count,
):
    padded = padded_2(psi_old, (("bulk", 2),), 1)
    right_side = source - lateral[:, 0:1] * padded[:, :, :-2] - lateral[:, 1:2] * padded[:, :, 2:]
    zero_state = jnp.zeros(source.shape[1:], jnp.float32)
    identity = jnp.broadcast_to(
        jnp.eye(5, dtype=jnp.float32)[:, :, None, None], (5, 5) + source.shape[2:]
    )
    transfer, leaving = block_affine(right_side, lower_jac, diag_inv, identity, zero_state, False)
    boundary = zero_state
    for relay_step in range(lax.axis_size("sweep") - 1):
        boundary = from_behind(matvec(transfer, boundary) + leaving, "sweep", 1)
    forward_field = forward_sweep(right_side, lower_jac, diag_inv, boundary)
    transfer, leaving = block_affine(forward_field, upper_jac, diag_inv, identity, zero_state, True)
    boundary = zero_state
    for relay_step in range(lax.axis_size("sweep") - 1):
        boundary = from_behind(matvec(transfer, boundary) + leaving, "sweep", -1)
    adjoint = backward_sweep(forward_field, upper_jac, diag_inv, boundary)
    width_j = source.shape[2]
    width_k = source.shape[3]
    slots = face_cell.shape[0]
    plane_index = face_cell // (width_j * width_k)
    rest_index = face_cell % (width_j * width_k)
    column_index = rest_index // width_k
    depth_index = rest_index % width_k
    at_faces = adjoint[plane_index, :, column_index, depth_index]
    partial_value = jnp.sum(at_faces * face_weight.T, axis=1)
    active = jnp.arange(slots, dtype=jnp.int32) < face_count[0]
    partial_value = jnp.where(active, partial_value, jnp.float32(0.0))
    owner_dev = face_owner[:, 0]
    owners = lax.axis_size("bulk")
    dense_sums = jax.ops.segment_sum(
        partial_value, owner_dev * NODES_DEV + face_node, num_segments=NODES_DEV * owners
    )
    summed = lax.psum(dense_sums, ("sweep", "bulk"))
    node_sens = lax.dynamic_slice_in_dim(summed, lax.axis_index("bulk") * NODES_DEV, NODES_DEV)
    return (adjoint, node_sens)


def solution(mesh):
    placed = (
        P("sweep", None, "bulk", None),
        P("sweep", None, "bulk", None),
        P("sweep", None, "bulk", None),
        P("sweep", None, None, "bulk", None),
        P("sweep", None, None, "bulk", None),
        P("sweep", None, None, "bulk", None),
        P(None, ("sweep", "bulk")),
        P(("sweep", "bulk")),
        P(("sweep", "bulk"), None),
        P(("sweep", "bulk")),
        P(("sweep", "bulk")),
    )
    return jax.shard_map(
        per_device,
        mesh=mesh,
        in_specs=placed,
        out_specs=(P("sweep", None, "bulk", None), P("bulk")),
        check_vma=False,
    )
```

profile of v0, /device:TPU:0, one launch (start us, length us, event | category | flops | bytes accessed | tf_op | source)
XLA Modules:
  0.0 318.8 jit_solution(10096926136467632355)
XLA Ops:
  7.2 1.6 fusion.88
  8.8 5.0 %collective-permute-start = (f32[32,5,1,128]{3,0,2,1:T(8,128)S(1)}, f32[32,5,1,128]{3,0,2,1:T(8,128)S(1)}, u32[]{:S(2)}, u32[]{:S(2)}) collective-permute-start(f32[32,5,1,128]{3,0,2,1:T(8,128)S(1)} %copy.123), channel_id=1, source_target_pairs={{0,1},{1,2},{2,3},{3,4},{4,5},{5,6},{6,7},{8,9},{9,10},{10,11},{11... | collective-permute-start | bytes 245768 | tf_op jit(solution)/shard_map/ppermute | solution.py:16
  13.8 1.3 collective-permute-start.1
  16.1 2.0 slice_bitcast_fusion.92
  18.1 2.1 slice_bitcast_fusion.32
  21.2 1.0 slice-done.1
  22.7 1.6 slice-done.4
  41.3 1.5 collective-permute-start.2
  43.6 4.2 %collective-permute-start.3 = (f32[5,16,128]{2,1,0:T(8,128)S(1)}, f32[5,16,128]{2,1,0:T(8,128)S(1)}, u32[]{:S(2)}, u32[]{:S(2)}) collective-permute-start(f32[5,16,128]{2,1,0:T(8,128)S(1)} %add.57), channel_id=1, source_target_pairs={{0,8},{8,16},{16,24},{1,9},{9,17},{17,25},{2,10},{10,18},{18,26},{... | collective-permute-start | bytes 122888 | tf_op jit(solution)/shard_map/ppermute | solution.py:25
  48.7 4.5 %collective-permute-start.4 = (f32[5,16,128]{2,1,0:T(8,128)S(1)}, f32[5,16,128]{2,1,0:T(8,128)S(1)}, u32[]{:S(2)}, u32[]{:S(2)}) collective-permute-start(f32[5,16,128]{2,1,0:T(8,128)S(1)} %add.58), channel_id=1, source_target_pairs={{0,8},{8,16},{16,24},{1,9},{9,17},{17,25},{2,10},{10,18},{18,26},{... | collective-permute-start | bytes 122888 | tf_op jit(solution)/shard_map/ppermute | solution.py:25
  58.9 1.4 collective-permute-start.5
  60.4 3.9 %collective-permute-done.5 = f32[5,16,128]{2,1,0:T(8,128)S(1)} collective-permute-done((f32[5,16,128]{2,1,0:T(8,128)S(1)}, f32[5,16,128]{2,1,0:T(8,128)S(1)}, u32[]{:S(2)}, u32[]{:S(2)}) %collective-permute-start.5) | collective-permute-done | bytes 40992 | tf_op jit(solution)/shard_map/ppermute | solution.py:25
  64.3 1.3 collective-permute-start.6
  65.6 4.6 %collective-permute-done.6 = f32[5,16,128]{2,1,0:T(8,128)S(1)} collective-permute-done((f32[5,16,128]{2,1,0:T(8,128)S(1)}, f32[5,16,128]{2,1,0:T(8,128)S(1)}, u32[]{:S(2)}, u32[]{:S(2)}) %collective-permute-start.6) | collective-permute-done | bytes 40992 | tf_op jit(solution)/shard_map/ppermute | solution.py:25
  70.8 1.5 collective-permute-start.7
  72.4 1.2 copy.122
  75.0 1.5 collective-permute-done.7
  76.5 1.0 multiply_reduce_fusion.191
  77.5 1.1 multiply_reduce_fusion.190
  78.6 1.0 sub.1037
  79.6 1.0 multiply_reduce_fusion.189
  80.6 1.0 multiply_reduce_fusion.188
  82.3 1.0 multiply_reduce_fusion.187
  83.3 1.0 multiply_reduce_fusion.186
  85.1 1.0 multiply_reduce_fusion.185
  86.0 1.0 multiply_reduce_fusion.184
  87.8 1.0 multiply_reduce_fusion.183
  88.7 1.0 multiply_reduce_fusion.182
  90.5 1.0 multiply_reduce_fusion.181
  91.5 1.0 multiply_reduce_fusion.180
  93.2 1.0 multiply_reduce_fusion.179
  94.2 1.0 multiply_reduce_fusion.178
  95.9 1.0 multiply_reduce_fusion.177
  96.9 1.0 multiply_reduce_fusion.176
  98.7 1.0 multiply_reduce_fusion.175
  99.6 1.0 multiply_reduce_fusion.174
  101.4 1.0 multiply_reduce_fusion.173
  103.3 1.0 multiply_reduce_fusion.171
  104.3 1.0 multiply_reduce_fusion.170
  105.3 1.0 multiply_reduce_fusion.169
  107.3 1.0 multiply_reduce_fusion.165
  121.5 1.0 multiply_reduce_fusion.137
  123.5 1.0 multiply_reduce_fusion.133
  126.9 16.5 %copy.121 = f32[32,5,16,128]{1,3,2,0:T(8,128)} copy(f32[32,5,16,128]{3,2,1,0:T(8,128)S(1)} %constant_dynamic-update-slice_fusion) | data formatting | bytes 2621440 | tf_op jit(solution)/shard_map/concatenate | solution.py:56
  143.4 22.2 %gather_fusion = f32[2048,5]{1,0:T(8,128)S(1)} fusion(f32[32,5,16,128]{1,3,2,0:T(8,128)} %copy.121, s32[2048]{0:T(1024)S(1)} %fusion.74), kind=kCustom, calls=%fused_computation | custom fusion | bytes 106496 | tf_op jit(solution)/shard_map/gather | solution.py:120
  166.0 12.2 %scatter_custom_fusion = f32[131072]{0:T(1024)} fusion(s32[2048]{0:T(1024)} %add.62, f32[2048]{0:T(1024)S(1)} %fusion.81, f32[]{:T(128)} %constant.53.clone.1), kind=kCustom, calls=%fused_computation.138 | custom fusion | flops 2048 | bytes 524800 | tf_op jit(solution)/shard_map/scatter-add | solution.py:126
  178.2 132.3 %all-reduce.2.cloned.1.call-done = f32[131072]{0:T(1024)} async-done(((f32[131072]{0:T(1024)}), f32[131072]{0:T(1024)}) %all-reduce.2.cloned.1.call-update) | async-done | bytes 524304 | tf_op jit(solution)/shard_map/psum | solution.py:129
  310.5 1.5 dynamic_slice.3
  (736 shorter events, 49.8 us)
Async XLA Ops:
  7.2 303.3 %all-reduce.2.cloned.1.call-start = ((), (), s32[]{:S(2)}) async-start(), calls=%async_computation | async-start | bytes 1048576 | tf_op jit(solution)/shard_map/psum | solution.py:129
  7.2 13.0 %copy-start = (f32[32,5,5,16,128]{4,3,2,1,0:T(8,128)S(1)}, f32[32,5,5,16,128]{4,3,2,1,0:T(8,128)}, u32[]{:S(2)}) copy-start(f32[32,5,5,16,128]{4,3,2,1,0:T(8,128)} %param.15) | copy-start | bytes 19660804
  8.8 29.5 %collective-permute-start = (f32[32,5,1,128]{3,0,2,1:T(8,128)S(1)}, f32[32,5,1,128]{3,0,2,1:T(8,128)S(1)}, u32[]{:S(2)}, u32[]{:S(2)}) collective-permute-start(f32[32,5,1,128]{3,0,2,1:T(8,128)S(1)} %copy.123), channel_id=1, source_target_pairs={{0,1},{1,2},{2,3},{3,4},{4,5},{5,6},{6,7},{8,9},{9,10},{10,11},{11... | collective-permute-start | bytes 245768 | tf_op jit(solution)/shard_map/ppermute | solution.py:16
  13.8 24.5 %collective-permute-start.1 = (f32[32,5,1,128]{3,0,2,1:T(8,128)S(1)}, f32[32,5,1,128]{3,0,2,1:T(8,128)S(1)}, u32[]{:S(2)}, u32[]{:S(2)}) collective-permute-start(f32[32,5,1,128]{3,0,2,1:T(8,128)S(1)} %copy.124), channel_id=1, source_target_pairs={{1,0},{2,1},{3,2},{4,3},{5,4},{6,5},{7,6},{9,8},{10,9},{11,10},{12... | collective-permute-start | bytes 245768 | tf_op jit(solution)/shard_map/ppermute | solution.py:17
  18.1 3.1 slice-start
  22.4 3.1 copy-start.52
  41.3 2.3 collective-permute-start.2
  43.6 5.0 %collective-permute-start.3 = (f32[5,16,128]{2,1,0:T(8,128)S(1)}, f32[5,16,128]{2,1,0:T(8,128)S(1)}, u32[]{:S(2)}, u32[]{:S(2)}) collective-permute-start(f32[5,16,128]{2,1,0:T(8,128)S(1)} %add.57), channel_id=1, source_target_pairs={{0,8},{8,16},{16,24},{1,9},{9,17},{17,25},{2,10},{10,18},{18,26},{... | collective-permute-start | bytes 122888 | tf_op jit(solution)/shard_map/ppermute | solution.py:25
  48.7 5.3 %collective-permute-start.4 = (f32[5,16,128]{2,1,0:T(8,128)S(1)}, f32[5,16,128]{2,1,0:T(8,128)S(1)}, u32[]{:S(2)}, u32[]{:S(2)}) collective-permute-start(f32[5,16,128]{2,1,0:T(8,128)S(1)} %add.58), channel_id=1, source_target_pairs={{0,8},{8,16},{16,24},{1,9},{9,17},{17,25},{2,10},{10,18},{18,26},{... | collective-permute-start | bytes 122888 | tf_op jit(solution)/shard_map/ppermute | solution.py:25
  54.3 4.4 %copy-start.4 = (f32[5,16,128]{2,1,0:T(8,128)}, f32[5,16,128]{2,1,0:T(8,128)S(1)}, u32[]{:S(2)}) copy-start(f32[5,16,128]{2,1,0:T(8,128)S(1)} %multiply_reduce_fusion.315) | copy-start | bytes 122884
  54.4 4.2 %copy-start.6 = (f32[5,16,128]{2,1,0:T(8,128)}, f32[5,16,128]{2,1,0:T(8,128)S(1)}, u32[]{:S(2)}) copy-start(f32[5,16,128]{2,1,0:T(8,128)S(1)} %multiply_reduce_fusion.313) | copy-start | bytes 122884
  54.5 4.1 %copy-start.8 = (f32[5,16,128]{2,1,0:T(8,128)}, f32[5,16,128]{2,1,0:T(8,128)S(1)}, u32[]{:S(2)}) copy-start(f32[5,16,128]{2,1,0:T(8,128)S(1)} %multiply_reduce_fusion.311) | copy-start | bytes 122884
  54.5 3.9 %copy-start.10 = (f32[5,16,128]{2,1,0:T(8,128)}, f32[5,16,128]{2,1,0:T(8,128)S(1)}, u32[]{:S(2)}) copy-start(f32[5,16,128]{2,1,0:T(8,128)S(1)} %multiply_reduce_fusion.309) | copy-start | bytes 122884
  54.6 3.8 %copy-start.12 = (f32[5,16,128]{2,1,0:T(8,128)}, f32[5,16,128]{2,1,0:T(8,128)S(1)}, u32[]{:S(2)}) copy-start(f32[5,16,128]{2,1,0:T(8,128)S(1)} %multiply_reduce_fusion.307) | copy-start | bytes 122884
  54.7 3.6 %copy-start.14 = (f32[5,16,128]{2,1,0:T(8,128)}, f32[5,16,128]{2,1,0:T(8,128)S(1)}, u32[]{:S(2)}) copy-start(f32[5,16,128]{2,1,0:T(8,128)S(1)} %multiply_reduce_fusion.305) | copy-start | bytes 122884
  54.8 3.5 %copy-start.16 = (f32[5,16,128]{2,1,0:T(8,128)}, f32[5,16,128]{2,1,0:T(8,128)S(1)}, u32[]{:S(2)}) copy-start(f32[5,16,128]{2,1,0:T(8,128)S(1)} %multiply_reduce_fusion.303) | copy-start | bytes 122884
  54.9 3.3 %copy-start.18 = (f32[5,16,128]{2,1,0:T(8,128)}, f32[5,16,128]{2,1,0:T(8,128)S(1)}, u32[]{:S(2)}) copy-start(f32[5,16,128]{2,1,0:T(8,128)S(1)} %multiply_reduce_fusion.301) | copy-start | bytes 122884
  54.9 3.1 copy-start.20
  55.0 3.0 copy-start.22
  57.4 8.1 %copy-start.55 = (s32[2048,1]{0,1:T(1,128)S(1)}, s32[2048,1]{0,1:T(1,128)}, u32[]{:S(2)}) copy-start(s32[2048,1]{0,1:T(1,128)} %param.19) | copy-start | bytes 24580
  57.5 14.9 %copy-start.56 = (s32[2048]{0:T(1024)S(1)}, s32[2048]{0:T(1024)}, u32[]{:S(2)}) copy-start(s32[2048]{0:T(1024)} %param.18) | copy-start | bytes 24580
  57.7 16.8 %copy-start.54 = (s32[2048]{0:T(1024)S(1)}, s32[2048]{0:T(1024)}, u32[]{:S(2)}) copy-start(s32[2048]{0:T(1024)} %param.20) | copy-start | bytes 24580
  58.4 47.8 %slice-start.2 = ((s8[6553600]{0:T(1024)(128)(4,1)}), s8[2359296]{0:T(1024)(128)(4,1)S(1)}, s32[]{:S(2)}) async-start(s8[6553600]{0:T(1024)(128)(4,1)} %bitcast.1165), calls=%async_computation.3 | async-start | bytes 4718592
  58.9 5.3 %collective-permute-start.5 = (f32[5,16,128]{2,1,0:T(8,128)S(1)}, f32[5,16,128]{2,1,0:T(8,128)S(1)}, u32[]{:S(2)}, u32[]{:S(2)}) collective-permute-start(f32[5,16,128]{2,1,0:T(8,128)S(1)} %get-tuple-element.10), channel_id=1, source_target_pairs={{8,0},{16,8},{24,16},{9,1},{17,9},{25,17},{10,2},{18,10},{26,18},{... | collective-permute-start | bytes 122888 | tf_op jit(solution)/shard_map/ppermute | solution.py:25
  64.3 5.9 %collective-permute-start.6 = (f32[5,16,128]{2,1,0:T(8,128)S(1)}, f32[5,16,128]{2,1,0:T(8,128)S(1)}, u32[]{:S(2)}, u32[]{:S(2)}) collective-permute-start(f32[5,16,128]{2,1,0:T(8,128)S(1)} %add.60), channel_id=1, source_target_pairs={{8,0},{16,8},{24,16},{9,1},{17,9},{25,17},{10,2},{18,10},{26,18},{... | collective-permute-start | bytes 122888 | tf_op jit(solution)/shard_map/ppermute | solution.py:25
  70.8 5.7 %collective-permute-start.7 = (f32[5,16,128]{2,1,0:T(8,128)}, f32[5,16,128]{2,1,0:T(8,128)}, u32[]{:S(2)}, u32[]{:S(2)}) collective-permute-start(f32[5,16,128]{2,1,0:T(8,128)} %add.61), channel_id=1, source_target_pairs={{8,0},{16,8},{24,16},{9,1},{17,9},{25,17},{10,2},{18,10},{26,18},{... | collective-permute-start | bytes 122888 | tf_op jit(solution)/shard_map/ppermute | solution.py:25
  73.6 29.7 %copy-start.43 = (f32[5,16,128]{2,1,0:T(8,128)S(1)}, f32[5,16,128]{2,1,0:T(8,128)}, u32[]{:S(2)}) copy-start(f32[5,16,128]{2,1,0:T(8,128)} %copy-done.42) | copy-start | bytes 122884
  73.6 31.6 %copy-start.41 = (f32[5,16,128]{2,1,0:T(8,128)S(1)}, f32[5,16,128]{2,1,0:T(8,128)}, u32[]{:S(2)}) copy-start(f32[5,16,128]{2,1,0:T(8,128)} %copy-done.40) | copy-start | bytes 122884
  73.6 32.7 %copy-start.39 = (f32[5,16,128]{2,1,0:T(8,128)S(1)}, f32[5,16,128]{2,1,0:T(8,128)}, u32[]{:S(2)}) copy-start(f32[5,16,128]{2,1,0:T(8,128)} %copy-done.38) | copy-start | bytes 122884
  73.6 33.7 %copy-start.37 = (f32[5,16,128]{2,1,0:T(8,128)S(1)}, f32[5,16,128]{2,1,0:T(8,128)}, u32[]{:S(2)}) copy-start(f32[5,16,128]{2,1,0:T(8,128)} %copy-done.36) | copy-start | bytes 122884
  73.6 34.7 %copy-start.35 = (f32[5,16,128]{2,1,0:T(8,128)S(1)}, f32[5,16,128]{2,1,0:T(8,128)}, u32[]{:S(2)}) copy-start(f32[5,16,128]{2,1,0:T(8,128)} %copy-done.34) | copy-start | bytes 122884
  73.7 35.7 %copy-start.33 = (f32[5,16,128]{2,1,0:T(8,128)S(1)}, f32[5,16,128]{2,1,0:T(8,128)}, u32[]{:S(2)}) copy-start(f32[5,16,128]{2,1,0:T(8,128)} %copy-done.32) | copy-start | bytes 122884
  73.7 36.7 %copy-start.31 = (f32[5,16,128]{2,1,0:T(8,128)S(1)}, f32[5,16,128]{2,1,0:T(8,128)}, u32[]{:S(2)}) copy-start(f32[5,16,128]{2,1,0:T(8,128)} %copy-done.30) | copy-start | bytes 122884
  73.7 37.7 %copy-start.29 = (f32[5,16,128]{2,1,0:T(8,128)S(1)}, f32[5,16,128]{2,1,0:T(8,128)}, u32[]{:S(2)}) copy-start(f32[5,16,128]{2,1,0:T(8,128)} %copy-done.28) | copy-start | bytes 122884
  73.7 38.7 %copy-start.27 = (f32[5,16,128]{2,1,0:T(8,128)S(1)}, f32[5,16,128]{2,1,0:T(8,128)}, u32[]{:S(2)}) copy-start(f32[5,16,128]{2,1,0:T(8,128)} %copy-done.26) | copy-start | bytes 122884
  75.0 38.3 %copy-start.25 = (f32[5,16,128]{2,1,0:T(8,128)S(1)}, f32[5,16,128]{2,1,0:T(8,128)}, u32[]{:S(2)}) copy-start(f32[5,16,128]{2,1,0:T(8,128)} %copy-done.24) | copy-start | bytes 122884
  77.5 28.8 %slice-start.3 = ((s8[6553600]{0:T(1024)(128)(4,1)}), s8[4194304]{0:T(1024)(128)(4,1)S(1)}, s32[]{:S(2)}) async-start(s8[6553600]{0:T(1024)(128)(4,1)} %bitcast.1165), calls=%async_computation.4 | async-start | bytes 8388608
  79.6 34.7 %copy-start.23 = (f32[5,16,128]{2,1,0:T(8,128)S(1)}, f32[5,16,128]{2,1,0:T(8,128)}, u32[]{:S(2)}) copy-start(f32[5,16,128]{2,1,0:T(8,128)} %copy-done.22) | copy-start | bytes 122884
  82.3 33.0 %copy-start.21 = (f32[5,16,128]{2,1,0:T(8,128)S(1)}, f32[5,16,128]{2,1,0:T(8,128)}, u32[]{:S(2)}) copy-start(f32[5,16,128]{2,1,0:T(8,128)} %copy-done.20) | copy-start | bytes 122884
  85.1 31.3 %copy-start.19 = (f32[5,16,128]{2,1,0:T(8,128)S(1)}, f32[5,16,128]{2,1,0:T(8,128)}, u32[]{:S(2)}) copy-start(f32[5,16,128]{2,1,0:T(8,128)} %copy-done.18) | copy-start | bytes 122884
  87.8 29.6 %copy-start.17 = (f32[5,16,128]{2,1,0:T(8,128)S(1)}, f32[5,16,128]{2,1,0:T(8,128)}, u32[]{:S(2)}) copy-start(f32[5,16,128]{2,1,0:T(8,128)} %copy-done.16) | copy-start | bytes 122884
  90.5 27.9 %copy-start.15 = (f32[5,16,128]{2,1,0:T(8,128)S(1)}, f32[5,16,128]{2,1,0:T(8,128)}, u32[]{:S(2)}) copy-start(f32[5,16,128]{2,1,0:T(8,128)} %copy-done.14) | copy-start | bytes 122884
  93.2 26.2 %copy-start.13 = (f32[5,16,128]{2,1,0:T(8,128)S(1)}, f32[5,16,128]{2,1,0:T(8,128)}, u32[]{:S(2)}) copy-start(f32[5,16,128]{2,1,0:T(8,128)} %copy-done.12) | copy-start | bytes 122884
  95.9 24.5 %copy-start.11 = (f32[5,16,128]{2,1,0:T(8,128)S(1)}, f32[5,16,128]{2,1,0:T(8,128)}, u32[]{:S(2)}) copy-start(f32[5,16,128]{2,1,0:T(8,128)} %copy-done.10) | copy-start | bytes 122884
  98.7 22.8 %copy-start.9 = (f32[5,16,128]{2,1,0:T(8,128)S(1)}, f32[5,16,128]{2,1,0:T(8,128)}, u32[]{:S(2)}) copy-start(f32[5,16,128]{2,1,0:T(8,128)} %copy-done.8) | copy-start | bytes 122884
  101.4 21.1 %copy-start.7 = (f32[5,16,128]{2,1,0:T(8,128)S(1)}, f32[5,16,128]{2,1,0:T(8,128)}, u32[]{:S(2)}) copy-start(f32[5,16,128]{2,1,0:T(8,128)} %copy-done.6) | copy-start | bytes 122884
  103.3 20.1 %copy-start.5 = (f32[5,16,128]{2,1,0:T(8,128)S(1)}, f32[5,16,128]{2,1,0:T(8,128)}, u32[]{:S(2)}) copy-start(f32[5,16,128]{2,1,0:T(8,128)} %copy-done.4) | copy-start | bytes 122884
  126.9 16.5 %copy-start.2 = (f32[32,5,16,128]{3,2,1,0:T(8,128)}, f32[32,5,16,128]{3,2,1,0:T(8,128)S(1)}, u32[]{:S(2)}) copy-start(f32[32,5,16,128]{3,2,1,0:T(8,128)S(1)} %constant_dynamic-update-slice_fusion) | copy-start | bytes 3932164
  (24 other events, 44.6 us)
Sparse Core Ops, SparseCore 0:
  178.3 132.1 all-reduce.1
where the time goes:
time: 321 us; the launch traced here: 319 us
  waiting for transfers between devices  145 us (45%)
  other arithmetic  81.3 us (25%)
  local copies, waits for them, and re-layouts  52.9 us (16%)
  starting transfers between devices  20.7 us (6%)
  between operations  19.2 us (6%)
    psum x1, waiting for transfers between devices, per_device(): summed = lax.psum(dense_sums, ('sweep', 'bulk'))  132 us
    reduce_sum x260, other arithmetic, matvec(): return jnp.sum(matrix * vector[None], axis=1)  46.8 us
    gather x1, local copies, waits for them, and re-layouts, per_device(): at_faces = adjoint[plane_index, :, column_index, depth_index]  22.2 us
    concatenate x2, local copies, waits for them, and re-layouts, backward_sweep(): lax.scan(backward_advance, start, (forward_field, upper_jac, diag_inv), r...  16.5 us
    ppermute x6, starting transfers between devices, from_behind(): return lax.ppermute(value, axis, pairs)  14.3 us
    ppermute x6, waiting for transfers between devices, from_behind(): return lax.ppermute(value, axis, pairs)  12.4 us
    scatter-add x1, other arithmetic, per_device(): jax.ops.segment_sum(partial_value, owner_dev * NODES_DEV + face_node, num...  12.2 us
    reduce_sum x126, other arithmetic, matmat(): return jnp.sum(matrix[:, :, None] * other[None], axis=1)  10.7 us
  transfers between devices with their start and end apart: 9, of which 7 were waited for; matrix products, arithmetic and copies ran while one was open for 6% of the time, Pallas kernels for 0%

commit v1 on v0

--- a/solution.py
+++ b/solution.py
@@ -126,7 +126,7 @@
     dense_sums = jax.ops.segment_sum(
         partial_value, owner_dev * NODES_DEV + face_node, num_segments=NODES_DEV * owners
     )
-    summed = lax.psum(dense_sums, ("sweep", "bulk"))
+    summed = lax.psum(lax.psum(dense_sums, axis_name="bulk"), axis_name="sweep")
     node_sens = lax.dynamic_slice_in_dim(summed, lax.axis_index("bulk") * NODES_DEV, NODES_DEV)
     return (adjoint, node_sens)
 

time: 321 us -> 300 us (0.935)
  waiting for transfers between devices: 145 us -> 124 us
    psum x1 -> x2, waiting for transfers between devices: 132 us -> 112 us  [per_device(): summed = lax.psum(lax.psum(dense_sums, axis_name='bulk'), axis_name='sweep')]
  transfers between devices with their start and end apart: 9 -> 10, of which waited for: 7 -> 8; matrix products, arithmetic and copies ran while one was open for 6% -> 7% of each run, Pallas kernels for 0% -> 0%
where the time goes in v1:
time: 300 us; the launch traced here: 298 us
  waiting for transfers between devices  124 us (41%)
  other arithmetic  81.4 us (27%)
  local copies, waits for them, and re-layouts  52.9 us (18%)
  starting transfers between devices  20.7 us (7%)
  between operations  19.2 us (6%)
    psum x2, waiting for transfers between devices, per_device(): summed = lax.psum(lax.psum(dense_sums, axis_name='bulk'), axis_name='sweep')  112 us
    reduce_sum x260, other arithmetic, matvec(): return jnp.sum(matrix * vector[None], axis=1)  46.8 us
    gather x1, local copies, waits for them, and re-layouts, per_device(): at_faces = adjoint[plane_index, :, column_index, depth_index]  22.2 us
    concatenate x2, local copies, waits for them, and re-layouts, backward_sweep(): lax.scan(backward_advance, start, (forward_field, upper_jac, diag_inv), r...  16.5 us
    ppermute x6, starting transfers between devices, from_behind(): return lax.ppermute(value, axis, pairs)  14.3 us
    ppermute x6, waiting for transfers between devices, from_behind(): return lax.ppermute(value, axis, pairs)  12.4 us
    scatter-add x1, other arithmetic, per_device(): jax.ops.segment_sum(partial_value, owner_dev * NODES_DEV + face_node, num...  12.2 us
    reduce_sum x126, other arithmetic, matmat(): return jnp.sum(matrix[:, :, None] * other[None], axis=1)  10.7 us
  transfers between devices with their start and end apart: 10, of which 8 were waited for; matrix products, arithmetic and copies ran while one was open for 7% of the time, Pallas kernels for 0%

profile of v1, /device:TPU:0, one launch (start us, length us, event | category | flops | bytes accessed | tf_op | source)
XLA Modules:
  0.0 298.3 jit_solution(6646469095780531807)
XLA Ops:
  7.2 1.6 fusion.88
  8.8 5.0 %collective-permute-start = (f32[32,5,1,128]{3,0,2,1:T(8,128)S(1)}, f32[32,5,1,128]{3,0,2,1:T(8,128)S(1)}, u32[]{:S(2)}, u32[]{:S(2)}) collective-permute-start(f32[32,5,1,128]{3,0,2,1:T(8,128)S(1)} %copy.123), channel_id=1, source_target_pairs={{0,1},{1,2},{2,3},{3,4},{4,5},{5,6},{6,7},{8,9},{9,10},{10,11},{11... | collective-permute-start | bytes 245768 | tf_op jit(solution)/shard_map/ppermute | solution.py:16
  13.8 1.3 collective-permute-start.1
  16.1 2.0 slice_bitcast_fusion.92
  18.1 2.1 slice_bitcast_fusion.32
  21.2 1.0 slice-done.1
  22.7 1.6 slice-done.4
  41.3 1.5 collective-permute-start.2
  43.6 4.2 %collective-permute-start.3 = (f32[5,16,128]{2,1,0:T(8,128)S(1)}, f32[5,16,128]{2,1,0:T(8,128)S(1)}, u32[]{:S(2)}, u32[]{:S(2)}) collective-permute-start(f32[5,16,128]{2,1,0:T(8,128)S(1)} %add.59), channel_id=1, source_target_pairs={{0,8},{8,16},{16,24},{1,9},{9,17},{17,25},{2,10},{10,18},{18,26},{... | collective-permute-start | bytes 122888 | tf_op jit(solution)/shard_map/ppermute | solution.py:25
  48.7 4.5 %collective-permute-start.4 = (f32[5,16,128]{2,1,0:T(8,128)S(1)}, f32[5,16,128]{2,1,0:T(8,128)S(1)}, u32[]{:S(2)}, u32[]{:S(2)}) collective-permute-start(f32[5,16,128]{2,1,0:T(8,128)S(1)} %add.60), channel_id=1, source_target_pairs={{0,8},{8,16},{16,24},{1,9},{9,17},{17,25},{2,10},{10,18},{18,26},{... | collective-permute-start | bytes 122888 | tf_op jit(solution)/shard_map/ppermute | solution.py:25
  58.9 1.4 collective-permute-start.5
  60.4 3.9 %collective-permute-done.5 = f32[5,16,128]{2,1,0:T(8,128)S(1)} collective-permute-done((f32[5,16,128]{2,1,0:T(8,128)S(1)}, f32[5,16,128]{2,1,0:T(8,128)S(1)}, u32[]{:S(2)}, u32[]{:S(2)}) %collective-permute-start.5) | collective-permute-done | bytes 40992 | tf_op jit(solution)/shard_map/ppermute | solution.py:25
  64.3 1.3 collective-permute-start.6
  65.6 4.6 %collective-permute-done.6 = f32[5,16,128]{2,1,0:T(8,128)S(1)} collective-permute-done((f32[5,16,128]{2,1,0:T(8,128)S(1)}, f32[5,16,128]{2,1,0:T(8,128)S(1)}, u32[]{:S(2)}, u32[]{:S(2)}) %collective-permute-start.6) | collective-permute-done | bytes 40992 | tf_op jit(solution)/shard_map/ppermute | solution.py:25
  70.8 1.5 collective-permute-start.7
  72.4 1.2 copy.122
  75.0 1.5 collective-permute-done.7
  76.5 1.0 multiply_reduce_fusion.191
  77.5 1.1 multiply_reduce_fusion.190
  78.6 1.0 sub.1037
  79.6 1.0 multiply_reduce_fusion.189
  80.6 1.0 multiply_reduce_fusion.188
  82.3 1.0 multiply_reduce_fusion.187
  83.3 1.0 multiply_reduce_fusion.186
  85.1 1.0 multiply_reduce_fusion.185
  86.0 1.0 multiply_reduce_fusion.184
  87.8 1.0 multiply_reduce_fusion.183
  88.7 1.0 multiply_reduce_fusion.182
  90.5 1.0 multiply_reduce_fusion.181
  91.5 1.0 multiply_reduce_fusion.180
  93.2 1.0 multiply_reduce_fusion.179
  94.2 1.0 multiply_reduce_fusion.178
  95.9 1.0 multiply_reduce_fusion.177
  96.9 1.0 multiply_reduce_fusion.176
  98.7 1.0 multiply_reduce_fusion.175
  99.6 1.0 multiply_reduce_fusion.174
  101.4 1.0 multiply_reduce_fusion.173
  103.3 1.0 multiply_reduce_fusion.171
  104.3 1.0 multiply_reduce_fusion.170
  105.3 1.0 multiply_reduce_fusion.169
  121.5 1.0 multiply_reduce_fusion.137
  123.5 1.0 multiply_reduce_fusion.133
  126.9 16.5 %copy.121 = f32[32,5,16,128]{1,3,2,0:T(8,128)} copy(f32[32,5,16,128]{3,2,1,0:T(8,128)S(1)} %constant_dynamic-update-slice_fusion) | data formatting | bytes 2621440 | tf_op jit(solution)/shard_map/concatenate | solution.py:56
  143.4 22.2 %gather_fusion = f32[2048,5]{1,0:T(8,128)S(1)} fusion(f32[32,5,16,128]{1,3,2,0:T(8,128)} %copy.121, s32[2048]{0:T(1024)S(1)} %fusion.74), kind=kCustom, calls=%fused_computation | custom fusion | bytes 106496 | tf_op jit(solution)/shard_map/gather | solution.py:120
  166.0 12.2 %scatter_custom_fusion = f32[131072]{0:T(1024)} fusion(s32[2048]{0:T(1024)} %add.64, f32[2048]{0:T(1024)S(1)} %fusion.81, f32[]{:T(128)} %constant.53.clone.1), kind=kCustom, calls=%fused_computation.138 | custom fusion | flops 2048 | bytes 524800 | tf_op jit(solution)/shard_map/scatter-add | solution.py:126
  178.2 76.8 %all-reduce.3.cloned.1.call-done = f32[131072]{0:T(1024)} async-done(((f32[131072]{0:T(1024)}), f32[131072]{0:T(1024)}) %all-reduce.3.cloned.1.call-update) | async-done | bytes 524304 | tf_op jit(solution)/shard_map/psum | solution.py:129
  255.0 34.9 %all-reduce.5.cloned.1.call-done = f32[131072]{0:T(1024)} async-done(((f32[131072]{0:T(1024)}), f32[131072]{0:T(1024)}) %all-reduce.5.cloned.1.call-update) | async-done | bytes 524304 | tf_op jit(solution)/shard_map/psum | solution.py:129
  290.0 1.5 dynamic_slice.3
  (739 shorter events, 50.8 us)
Async XLA Ops:
  7.2 247.8 %all-reduce.3.cloned.1.call-start = ((), (), s32[]{:S(2)}) async-start(), calls=%async_computation | async-start | bytes 1048576 | tf_op jit(solution)/shard_map/psum | solution.py:129
  7.2 13.0 %copy-start = (f32[32,5,5,16,128]{4,3,2,1,0:T(8,128)S(1)}, f32[32,5,5,16,128]{4,3,2,1,0:T(8,128)}, u32[]{:S(2)}) copy-start(f32[32,5,5,16,128]{4,3,2,1,0:T(8,128)} %param.15) | copy-start | bytes 19660804
  8.8 29.5 %collective-permute-start = (f32[32,5,1,128]{3,0,2,1:T(8,128)S(1)}, f32[32,5,1,128]{3,0,2,1:T(8,128)S(1)}, u32[]{:S(2)}, u32[]{:S(2)}) collective-permute-start(f32[32,5,1,128]{3,0,2,1:T(8,128)S(1)} %copy.123), channel_id=1, source_target_pairs={{0,1},{1,2},{2,3},{3,4},{4,5},{5,6},{6,7},{8,9},{9,10},{10,11},{11... | collective-permute-start | bytes 245768 | tf_op jit(solution)/shard_map/ppermute | solution.py:16
  13.8 24.5 %collective-permute-start.1 = (f32[32,5,1,128]{3,0,2,1:T(8,128)S(1)}, f32[32,5,1,128]{3,0,2,1:T(8,128)S(1)}, u32[]{:S(2)}, u32[]{:S(2)}) collective-permute-start(f32[32,5,1,128]{3,0,2,1:T(8,128)S(1)} %copy.124), channel_id=1, source_target_pairs={{1,0},{2,1},{3,2},{4,3},{5,4},{6,5},{7,6},{9,8},{10,9},{11,10},{12... | collective-permute-start | bytes 245768 | tf_op jit(solution)/shard_map/ppermute | solution.py:17
  18.1 3.1 %slice-start = ((s8[6553600]{0:T(1024)(128)(4,1)}), s8[4194304]{0:T(1024)(128)(4,1)S(1)}, s32[]{:S(2)}) async-start(s8[6553600]{0:T(1024)(128)(4,1)} %bitcast.1163), calls=%async_computation.2 | async-start | bytes 8388608
  22.4 3.1 %copy-start.52 = (f32[32,2,16,128]{3,2,1,0:T(8,128)S(1)}, f32[32,2,16,128]{3,2,1,0:T(8,128)}, u32[]{:S(2)}) copy-start(f32[32,2,16,128]{3,2,1,0:T(8,128)} %param.13) | copy-start | bytes 1572868
  41.3 2.3 collective-permute-start.2
  43.6 5.0 %collective-permute-start.3 = (f32[5,16,128]{2,1,0:T(8,128)S(1)}, f32[5,16,128]{2,1,0:T(8,128)S(1)}, u32[]{:S(2)}, u32[]{:S(2)}) collective-permute-start(f32[5,16,128]{2,1,0:T(8,128)S(1)} %add.59), channel_id=1, source_target_pairs={{0,8},{8,16},{16,24},{1,9},{9,17},{17,25},{2,10},{10,18},{18,26},{... | collective-permute-start | bytes 122888 | tf_op jit(solution)/shard_map/ppermute | solution.py:25
  48.7 5.3 %collective-permute-start.4 = (f32[5,16,128]{2,1,0:T(8,128)S(1)}, f32[5,16,128]{2,1,0:T(8,128)S(1)}, u32[]{:S(2)}, u32[]{:S(2)}) collective-permute-start(f32[5,16,128]{2,1,0:T(8,128)S(1)} %add.60), channel_id=1, source_target_pairs={{0,8},{8,16},{16,24},{1,9},{9,17},{17,25},{2,10},{10,18},{18,26},{... | collective-permute-start | bytes 122888 | tf_op jit(solution)/shard_map/ppermute | solution.py:25
  54.3 4.4 %copy-start.4 = (f32[5,16,128]{2,1,0:T(8,128)}, f32[5,16,128]{2,1,0:T(8,128)S(1)}, u32[]{:S(2)}) copy-start(f32[5,16,128]{2,1,0:T(8,128)S(1)} %multiply_reduce_fusion.315) | copy-start | bytes 122884
  54.4 4.2 %copy-start.6 = (f32[5,16,128]{2,1,0:T(8,128)}, f32[5,16,128]{2,1,0:T(8,128)S(1)}, u32[]{:S(2)}) copy-start(f32[5,16,128]{2,1,0:T(8,128)S(1)} %multiply_reduce_fusion.313) | copy-start | bytes 122884
  54.5 4.1 %copy-start.8 = (f32[5,16,128]{2,1,0:T(8,128)}, f32[5,16,128]{2,1,0:T(8,128)S(1)}, u32[]{:S(2)}) copy-start(f32[5,16,128]{2,1,0:T(8,128)S(1)} %multiply_reduce_fusion.311) | copy-start | bytes 122884
  54.5 3.9 %copy-start.10 = (f32[5,16,128]{2,1,0:T(8,128)}, f32[5,16,128]{2,1,0:T(8,128)S(1)}, u32[]{:S(2)}) copy-start(f32[5,16,128]{2,1,0:T(8,128)S(1)} %multiply_reduce_fusion.309) | copy-start | bytes 122884
  54.6 3.8 %copy-start.12 = (f32[5,16,128]{2,1,0:T(8,128)}, f32[5,16,128]{2,1,0:T(8,128)S(1)}, u32[]{:S(2)}) copy-start(f32[5,16,128]{2,1,0:T(8,128)S(1)} %multiply_reduce_fusion.307) | copy-start | bytes 122884
  54.7 3.6 %copy-start.14 = (f32[5,16,128]{2,1,0:T(8,128)}, f32[5,16,128]{2,1,0:T(8,128)S(1)}, u32[]{:S(2)}) copy-start(f32[5,16,128]{2,1,0:T(8,128)S(1)} %multiply_reduce_fusion.305) | copy-start | bytes 122884
  54.8 3.5 %copy-start.16 = (f32[5,16,128]{2,1,0:T(8,128)}, f32[5,16,128]{2,1,0:T(8,128)S(1)}, u32[]{:S(2)}) copy-start(f32[5,16,128]{2,1,0:T(8,128)S(1)} %multiply_reduce_fusion.303) | copy-start | bytes 122884
  54.9 3.3 %copy-start.18 = (f32[5,16,128]{2,1,0:T(8,128)}, f32[5,16,128]{2,1,0:T(8,128)S(1)}, u32[]{:S(2)}) copy-start(f32[5,16,128]{2,1,0:T(8,128)S(1)} %multiply_reduce_fusion.301) | copy-start | bytes 122884
  54.9 3.1 %copy-start.20 = (f32[5,16,128]{2,1,0:T(8,128)}, f32[5,16,128]{2,1,0:T(8,128)S(1)}, u32[]{:S(2)}) copy-start(f32[5,16,128]{2,1,0:T(8,128)S(1)} %multiply_reduce_fusion.299) | copy-start | bytes 122884
  57.4 8.1 %copy-start.55 = (s32[2048,1]{0,1:T(1,128)S(1)}, s32[2048,1]{0,1:T(1,128)}, u32[]{:S(2)}) copy-start(s32[2048,1]{0,1:T(1,128)} %param.19) | copy-start | bytes 24580
  57.5 14.9 %copy-start.56 = (s32[2048]{0:T(1024)S(1)}, s32[2048]{0:T(1024)}, u32[]{:S(2)}) copy-start(s32[2048]{0:T(1024)} %param.18) | copy-start | bytes 24580
  57.7 16.8 %copy-start.54 = (s32[2048]{0:T(1024)S(1)}, s32[2048]{0:T(1024)}, u32[]{:S(2)}) copy-start(s32[2048]{0:T(1024)} %param.20) | copy-start | bytes 24580
  58.4 47.8 %slice-start.2 = ((s8[6553600]{0:T(1024)(128)(4,1)}), s8[2359296]{0:T(1024)(128)(4,1)S(1)}, s32[]{:S(2)}) async-start(s8[6553600]{0:T(1024)(128)(4,1)} %bitcast.1165), calls=%async_computation.4 | async-start | bytes 4718592
  58.9 5.3 %collective-permute-start.5 = (f32[5,16,128]{2,1,0:T(8,128)S(1)}, f32[5,16,128]{2,1,0:T(8,128)S(1)}, u32[]{:S(2)}, u32[]{:S(2)}) collective-permute-start(f32[5,16,128]{2,1,0:T(8,128)S(1)} %get-tuple-element.10), channel_id=1, source_target_pairs={{8,0},{16,8},{24,16},{9,1},{17,9},{25,17},{10,2},{18,10},{26,18},{... | collective-permute-start | bytes 122888 | tf_op jit(solution)/shard_map/ppermute | solution.py:25
  64.3 5.9 %collective-permute-start.6 = (f32[5,16,128]{2,1,0:T(8,128)S(1)}, f32[5,16,128]{2,1,0:T(8,128)S(1)}, u32[]{:S(2)}, u32[]{:S(2)}) collective-permute-start(f32[5,16,128]{2,1,0:T(8,128)S(1)} %add.62), channel_id=1, source_target_pairs={{8,0},{16,8},{24,16},{9,1},{17,9},{25,17},{10,2},{18,10},{26,18},{... | collective-permute-start | bytes 122888 | tf_op jit(solution)/shard_map/ppermute | solution.py:25
  70.8 5.7 %collective-permute-start.7 = (f32[5,16,128]{2,1,0:T(8,128)}, f32[5,16,128]{2,1,0:T(8,128)}, u32[]{:S(2)}, u32[]{:S(2)}) collective-permute-start(f32[5,16,128]{2,1,0:T(8,128)} %add.63), channel_id=1, source_target_pairs={{8,0},{16,8},{24,16},{9,1},{17,9},{25,17},{10,2},{18,10},{26,18},{... | collective-permute-start | bytes 122888 | tf_op jit(solution)/shard_map/ppermute | solution.py:25
  73.6 29.7 %copy-start.43 = (f32[5,16,128]{2,1,0:T(8,128)S(1)}, f32[5,16,128]{2,1,0:T(8,128)}, u32[]{:S(2)}) copy-start(f32[5,16,128]{2,1,0:T(8,128)} %copy-done.42) | copy-start | bytes 122884
  73.6 31.6 %copy-start.41 = (f32[5,16,128]{2,1,0:T(8,128)S(1)}, f32[5,16,128]{2,1,0:T(8,128)}, u32[]{:S(2)}) copy-start(f32[5,16,128]{2,1,0:T(8,128)} %copy-done.40) | copy-start | bytes 122884
  73.6 32.7 %copy-start.39 = (f32[5,16,128]{2,1,0:T(8,128)S(1)}, f32[5,16,128]{2,1,0:T(8,128)}, u32[]{:S(2)}) copy-start(f32[5,16,128]{2,1,0:T(8,128)} %copy-done.38) | copy-start | bytes 122884
  73.6 33.7 %copy-start.37 = (f32[5,16,128]{2,1,0:T(8,128)S(1)}, f32[5,16,128]{2,1,0:T(8,128)}, u32[]{:S(2)}) copy-start(f32[5,16,128]{2,1,0:T(8,128)} %copy-done.36) | copy-start | bytes 122884
  73.6 34.7 %copy-start.35 = (f32[5,16,128]{2,1,0:T(8,128)S(1)}, f32[5,16,128]{2,1,0:T(8,128)}, u32[]{:S(2)}) copy-start(f32[5,16,128]{2,1,0:T(8,128)} %copy-done.34) | copy-start | bytes 122884
  73.7 35.7 %copy-start.33 = (f32[5,16,128]{2,1,0:T(8,128)S(1)}, f32[5,16,128]{2,1,0:T(8,128)}, u32[]{:S(2)}) copy-start(f32[5,16,128]{2,1,0:T(8,128)} %copy-done.32) | copy-start | bytes 122884
  73.7 36.7 %copy-start.31 = (f32[5,16,128]{2,1,0:T(8,128)S(1)}, f32[5,16,128]{2,1,0:T(8,128)}, u32[]{:S(2)}) copy-start(f32[5,16,128]{2,1,0:T(8,128)} %copy-done.30) | copy-start | bytes 122884
  73.7 37.7 %copy-start.29 = (f32[5,16,128]{2,1,0:T(8,128)S(1)}, f32[5,16,128]{2,1,0:T(8,128)}, u32[]{:S(2)}) copy-start(f32[5,16,128]{2,1,0:T(8,128)} %copy-done.28) | copy-start | bytes 122884
  73.7 38.7 %copy-start.27 = (f32[5,16,128]{2,1,0:T(8,128)S(1)}, f32[5,16,128]{2,1,0:T(8,128)}, u32[]{:S(2)}) copy-start(f32[5,16,128]{2,1,0:T(8,128)} %copy-done.26) | copy-start | bytes 122884
  75.0 38.3 %copy-start.25 = (f32[5,16,128]{2,1,0:T(8,128)S(1)}, f32[5,16,128]{2,1,0:T(8,128)}, u32[]{:S(2)}) copy-start(f32[5,16,128]{2,1,0:T(8,128)} %copy-done.24) | copy-start | bytes 122884
  77.5 28.8 %slice-start.3 = ((s8[6553600]{0:T(1024)(128)(4,1)}), s8[4194304]{0:T(1024)(128)(4,1)S(1)}, s32[]{:S(2)}) async-start(s8[6553600]{0:T(1024)(128)(4,1)} %bitcast.1165), calls=%async_computation.5 | async-start | bytes 8388608
  79.6 34.7 %copy-start.23 = (f32[5,16,128]{2,1,0:T(8,128)S(1)}, f32[5,16,128]{2,1,0:T(8,128)}, u32[]{:S(2)}) copy-start(f32[5,16,128]{2,1,0:T(8,128)} %copy-done.22) | copy-start | bytes 122884
  82.3 33.0 %copy-start.21 = (f32[5,16,128]{2,1,0:T(8,128)S(1)}, f32[5,16,128]{2,1,0:T(8,128)}, u32[]{:S(2)}) copy-start(f32[5,16,128]{2,1,0:T(8,128)} %copy-done.20) | copy-start | bytes 122884
  85.1 31.3 %copy-start.19 = (f32[5,16,128]{2,1,0:T(8,128)S(1)}, f32[5,16,128]{2,1,0:T(8,128)}, u32[]{:S(2)}) copy-start(f32[5,16,128]{2,1,0:T(8,128)} %copy-done.18) | copy-start | bytes 122884
  87.8 29.6 %copy-start.17 = (f32[5,16,128]{2,1,0:T(8,128)S(1)}, f32[5,16,128]{2,1,0:T(8,128)}, u32[]{:S(2)}) copy-start(f32[5,16,128]{2,1,0:T(8,128)} %copy-done.16) | copy-start | bytes 122884
  90.5 27.9 %copy-start.15 = (f32[5,16,128]{2,1,0:T(8,128)S(1)}, f32[5,16,128]{2,1,0:T(8,128)}, u32[]{:S(2)}) copy-start(f32[5,16,128]{2,1,0:T(8,128)} %copy-done.14) | copy-start | bytes 122884
  93.2 26.2 %copy-start.13 = (f32[5,16,128]{2,1,0:T(8,128)S(1)}, f32[5,16,128]{2,1,0:T(8,128)}, u32[]{:S(2)}) copy-start(f32[5,16,128]{2,1,0:T(8,128)} %copy-done.12) | copy-start | bytes 122884
  95.9 24.5 %copy-start.11 = (f32[5,16,128]{2,1,0:T(8,128)S(1)}, f32[5,16,128]{2,1,0:T(8,128)}, u32[]{:S(2)}) copy-start(f32[5,16,128]{2,1,0:T(8,128)} %copy-done.10) | copy-start | bytes 122884
  98.7 22.8 %copy-start.9 = (f32[5,16,128]{2,1,0:T(8,128)S(1)}, f32[5,16,128]{2,1,0:T(8,128)}, u32[]{:S(2)}) copy-start(f32[5,16,128]{2,1,0:T(8,128)} %copy-done.8) | copy-start | bytes 122884
  101.4 21.1 %copy-start.7 = (f32[5,16,128]{2,1,0:T(8,128)S(1)}, f32[5,16,128]{2,1,0:T(8,128)}, u32[]{:S(2)}) copy-start(f32[5,16,128]{2,1,0:T(8,128)} %copy-done.6) | copy-start | bytes 122884
  103.3 20.1 %copy-start.5 = (f32[5,16,128]{2,1,0:T(8,128)S(1)}, f32[5,16,128]{2,1,0:T(8,128)}, u32[]{:S(2)}) copy-start(f32[5,16,128]{2,1,0:T(8,128)} %copy-done.4) | copy-start | bytes 122884
  126.9 16.5 %copy-start.2 = (f32[32,5,16,128]{3,2,1,0:T(8,128)}, f32[32,5,16,128]{3,2,1,0:T(8,128)S(1)}, u32[]{:S(2)}) copy-start(f32[32,5,16,128]{3,2,1,0:T(8,128)S(1)} %constant_dynamic-update-slice_fusion) | copy-start | bytes 3932164
  178.2 111.8 %all-reduce.5.cloned.1.call-start = ((), (), s32[]{:S(2)}) async-start(), calls=%async_computation.1 | async-start | bytes 1048576 | tf_op jit(solution)/shard_map/psum | solution.py:129
  (25 other events, 47.6 us)
Sparse Core Ops, SparseCore 0:
  178.3 76.6 all-reduce.2
  257.5 32.4 all-reduce.4
